TPU v7x, 512 devices: a whole 4x4x16 slice. The times are simulated.
512 devices in a mesh: swath: 32 (over z, core), chan: 16 (over x, y).
Axes of the slice: x: 4, y: 4, z: 16, core: 2. Of those that a mesh axis runs over, the one named last changes fastest.
Arguments:
- grid_profiles: bfloat16 [32768, 256], P('swath'), may hold values from -6 to 6
- send_lists: int32 [32, 32, 128], P('swath'), may hold values from 0 to 1023
- counts: int32 [32, 32], P('swath'), may hold values from 1 to 128, as said below
- angle_index: int32 [128], replicated, may hold values from 0 to 7
- jacobian: bfloat16 [3, 256, 608], P(None, None, 'chan'), may hold values from -0.375 to 0.375
- observed: bfloat16 [608, 131072], P('chan', 'swath'), may hold values from -6 to 6
- kappa: float32 [2, 608], P(None, 'chan'), may hold values from 0.04 to 0.24
- factor: bfloat16 [608, 608], P('chan')
Outputs:
- weighted: float32 [608, 131072], P('chan', 'swath')
Inputs may be any that keep to these rules, and one draw needn't show every extreme that they name: `counts`: some receiver gets 128 live slots from every sender; every entry is at least one.
All inputs are finite; a program needn't handle non-finite values.
Results may differ from a plain program's by a relative error of at most 0.0029.
Values may be sent and summed in bfloat16 or wider, within the bound.
A program may use at most 64 MiB of HBM per device.

v0:
```python
import math
import jax
import jax.numpy as jnp
from jax import lax
from jax.sharding import PartitionSpec as P

XTRACK = 128
NANG = 8
max_zenith = math.pi / 3.0


def extended_2(block, sides, width):
    for axis, dim in sides:
        count = lax.axis_size(axis)
        forward = [(i, i + 1) for i in range(count - 1)]
        backward = [(target, source) for source, target in forward]
        low = lax.ppermute(
            lax.slice_in_dim(block, block.shape[dim] - width, None, axis=dim), axis, forward
        )
        high = lax.ppermute(lax.slice_in_dim(block, 0, width, axis=dim), axis, backward)
        block = jnp.concatenate([low, block, high], axis=dim)
    return block


def diffuse_once(extended, along_rate, cross_rate):
    center = extended[:, 1:-1]
    along_sum = extended[:, 2:] + extended[:, :-2] - 2.0 * center
    side_pad = jnp.pad(center, ((0, 0), (0, 0), (1, 1)))
    cross_sum = side_pad[:, :, 2:] + side_pad[:, :, :-2] - 2.0 * center
    return center + along_rate * along_sum + cross_rate * cross_sum


def line_rims(smooth_field):
    return extended_2(smooth_field, (("swath", 1),), 1)


def on_device(grid_profiles, send_lists, counts, angle_index, jacobian, observed, kappa, factor):
    slot_rows = send_lists[0]
    slots = slot_rows.shape[1]
    own_chan = observed.shape[0]
    pixel_count = observed.shape[1]
    line_count = pixel_count // XTRACK
    live_slot = jnp.arange(slots, dtype=jnp.int32)[None, :] < counts[0][:, None]
    zero_value = jnp.zeros((), grid_profiles.dtype)
    outgoing = jnp.where(live_slot[:, :, None], grid_profiles[slot_rows], zero_value)
    incoming = lax.all_to_all(outgoing, "swath", split_axis=0, concat_axis=0, tiled=True)
    pixel_profiles = incoming.reshape(pixel_count, grid_profiles.shape[1])
    model = jnp.einsum("mkc,pk->mcp", jacobian, pixel_profiles, preferred_element_type=jnp.float32)
    zenith = angle_index.astype(jnp.float32) * (max_zenith / (NANG - 1))
    slant_path = 1.0 / jnp.cos(zenith) - 1.0
    model = model.reshape(3, own_chan, line_count, XTRACK)
    departure = observed.astype(jnp.float32).reshape(own_chan, line_count, XTRACK) - (
        model[0] + slant_path * model[1] + slant_path * slant_path * model[2]
    )
    along_rate = kappa[0][:, None, None]
    cross_rate = kappa[1][:, None, None]
    smooth_field = departure
    for sweep in range(3):
        smooth_field = diffuse_once(line_rims(smooth_field), along_rate, cross_rate)
    smoothed = smooth_field.reshape(own_chan, pixel_count).astype(jnp.bfloat16)
    return jnp.dot(
        factor,
        lax.all_gather(smoothed, "chan", axis=0, tiled=True),
        preferred_element_type=jnp.float32,
    )


def solution(mesh):
    in_specs = (
        P("swath", None),
        P("swath", None, None),
        P("swath", None),
        P(),
        P(None, None, "chan"),
        P("chan", "swath"),
        P(None, "chan"),
        P("chan", None),
    )
    out_specs = P("chan", "swath")
    return jax.shard_map(
        on_device, mesh=mesh, in_specs=in_specs, out_specs=out_specs, check_vma=False
    )
```

profile of v0, /device:TPU:1, one launch (start us, length us, event | category | flops | bytes accessed | tf_op | source)
XLA Modules:
  0.0 252.0 jit_solution(1715933017502331585)
XLA Ops:
  6.5 0.0 copy-start
  6.5 0.8 iota_compare_fusion
  7.3 0.7 fusion.29
  8.0 0.0 copy-done
  8.1 14.6 %gather_fusion = bf16[4096,256]{1,0:T(8,128)(2,1)S(1)} fusion(bf16[1024,256]{1,0:T(8,128)(2,1)S(1)} %copy-done, s32[4096]{0:T(1024)S(1)} %fusion.29), kind=kCustom, calls=%fused_computation | custom fusion | bytes 4210688 | tf_op jit(solution)/shard_map/gather | solution.py:45
  22.7 1.7 broadcast_select_fusion
  24.4 0.0 copy-start.1
  24.4 16.9 %all-to-all-start = ((bf16[32,128,256]{2,1,0:T(8,128)(2,1)}), bf16[32,128,256]{2,1,0:T(8,128)(2,1)S(1)}, u32[]{:S(2)}, u32[]{:S(2)}) async-start(bf16[32,128,256]{2,1,0:T(8,128)(2,1)} %broadcast_select_fusion), calls=%async_computation | async-start | bytes 4194304 | tf_op jit(solution)/shard_map/all_to_all | solution.py:46
  41.2 0.0 copy-start.5
  41.3 0.0 copy-start.2
  41.3 0.0 all-gather.3.cloned.1.call-start
  41.3 0.0 copy-done.1
  41.4 0.1 copy.9
  41.5 0.4 copy-done.5
  42.0 97.9 %all-to-all-done = bf16[32,128,256]{2,1,0:T(8,128)(2,1)S(1)} async-done(((bf16[32,128,256]{2,1,0:T(8,128)(2,1)}), bf16[32,128,256]{2,1,0:T(8,128)(2,1)S(1)}, u32[]{:S(2)}, u32[]{:S(2)}) %all-to-all-start) | async-done | bytes 2097184 | tf_op jit(solution)/shard_map/all_to_all | solution.py:46
  139.9 0.0 copy-done.2
  139.9 0.8 convolution_bitcast_fusion
  140.7 0.2 fusion.31
  140.8 0.1 copy.10
  141.0 0.1 copy.12
  141.1 0.0 copy-start.4
  141.1 0.1 copy.11
  141.2 0.3 fusion.14
  141.6 2.8 %collective-permute-start = (f32[38,1,128]{2,1,0:T(1,128)S(1)}, f32[38,1,128]{2,1,0:T(1,128)S(1)}, u32[]{:S(2)}, u32[]{:S(2)}) collective-permute-start(f32[38,1,128]{2,1,0:T(1,128)S(1)} %get-tuple-element.14), channel_id=1, source_target_pairs={{16,0},{32,16},{48,32},{64,48},{80,64},{96,80},{112,96},{128,112},... | collective-permute-start | bytes 58376 | tf_op jit(solution)/shard_map/ppermute | solution.py:20
  144.3 4.2 %collective-permute-start.1 = (f32[38,1,128]{2,1,0:T(1,128)S(1)}, f32[38,1,128]{2,1,0:T(1,128)S(1)}, u32[]{:S(2)}, u32[]{:S(2)}) collective-permute-start(f32[38,1,128]{2,1,0:T(1,128)S(1)} %get-tuple-element.15), channel_id=1, source_target_pairs={{0,16},{16,32},{32,48},{48,64},{64,80},{80,96},{96,112},{112,128},... | collective-permute-start | bytes 58376 | tf_op jit(solution)/shard_map/ppermute | solution.py:17
  148.6 0.0 copy-done.4
  148.6 0.0 collective-permute-done
  148.6 0.8 collective-permute-done.1
  149.4 0.5 fusion.3
  150.0 1.9 collective-permute-start.2
  151.9 4.2 %collective-permute-start.3 = (f32[38,1,128]{2,1,0:T(1,128)S(1)}, f32[38,1,128]{2,1,0:T(1,128)S(1)}, u32[]{:S(2)}, u32[]{:S(2)}) collective-permute-start(f32[38,1,128]{2,1,0:T(1,128)S(1)} %get-tuple-element.13), channel_id=1, source_target_pairs={{0,16},{16,32},{32,48},{48,64},{64,80},{80,96},{96,112},{112,128},... | collective-permute-start | bytes 58376 | tf_op jit(solution)/shard_map/ppermute | solution.py:17
  156.2 0.0 collective-permute-done.2
  156.2 0.9 collective-permute-done.3
  157.0 0.5 fusion.7
  157.6 1.9 collective-permute-start.4
  159.5 4.2 %collective-permute-start.5 = (f32[38,1,128]{2,1,0:T(1,128)S(1)}, f32[38,1,128]{2,1,0:T(1,128)S(1)}, u32[]{:S(2)}, u32[]{:S(2)}) collective-permute-start(f32[38,1,128]{2,1,0:T(1,128)S(1)} %get-tuple-element.11), channel_id=1, source_target_pairs={{0,16},{16,32},{32,48},{48,64},{64,80},{80,96},{96,112},{112,128},... | collective-permute-start | bytes 58376 | tf_op jit(solution)/shard_map/ppermute | solution.py:17
  163.8 0.0 collective-permute-done.4
  163.8 0.9 collective-permute-done.5
  164.6 0.6 fusion.12
  165.2 0.9 reshape.88
  166.1 0.0 all-gather.3.cloned.1.call-update
  166.2 0.0 copy-start.3
  166.2 69.0 %all-gather.3.cloned.1.call-done = bf16[16,38,4096]{2,1,0:T(8,128)(2,1)} async-done(((bf16[1,38,4096]{2,1,0:T(8,128)(2,1)}), bf16[16,38,4096]{2,1,0:T(8,128)(2,1)}) %all-gather.3.cloned.1.call-update) | async-done | bytes 4980752 | tf_op jit(solution)/shard_map/all_gather | solution.py:63
  235.2 5.7 %reshape.89 = bf16[608,4096]{1,0:T(8,128)(2,1)} reshape(bf16[16,38,4096]{2,1,0:T(8,128)(2,1)} %all-gather.3.cloned.1.call-done) | data formatting | bytes 9961472
  240.9 0.0 copy-done.3
  240.9 4.2 %convolution_bitcast_fusion.1 = f32[38,4096]{1,0:T(8,128)} fusion(bf16[608,4096]{1,0:T(8,128)(2,1)} %reshape.89, bf16[38,608]{1,0:T(8,128)(2,1)S(1)} %copy-done.3), kind=kOutput, calls=%fused_computation.2 | convolution fusion | flops 189267968 | bytes 5649536 | tf_op jit(solution)/shard_map/dot_general | solution.py:61
  (6 shorter events, 0.2 us)
Async XLA Ops:
  6.5 1.5 copy-start
  24.4 17.0 %copy-start.1 = (bf16[38,4096]{1,0:T(8,128)(2,1)S(1)}, bf16[38,4096]{1,0:T(8,128)(2,1)}, u32[]{:S(2)}) copy-start(bf16[38,4096]{1,0:T(8,128)(2,1)} %param.13) | copy-start | bytes 933892
  24.4 115.5 %all-to-all-start = ((bf16[32,128,256]{2,1,0:T(8,128)(2,1)}), bf16[32,128,256]{2,1,0:T(8,128)(2,1)S(1)}, u32[]{:S(2)}, u32[]{:S(2)}) async-start(bf16[32,128,256]{2,1,0:T(8,128)(2,1)} %broadcast_select_fusion), calls=%async_computation | async-start | bytes 4194304 | tf_op jit(solution)/shard_map/all_to_all | solution.py:46
  41.2 0.7 copy-start.5
  41.3 98.6 %copy-start.2 = (bf16[3,256,38]{1,2,0:T(8,128)(2,1)S(1)}, bf16[3,256,38]{1,2,0:T(8,128)(2,1)}, u32[]{:S(2)}) copy-start(bf16[3,256,38]{1,2,0:T(8,128)(2,1)} %param.12) | copy-start | bytes 175108
  41.3 193.9 %all-gather.3.cloned.1.call-start = ((), (), s32[]{:S(2)}) async-start(), calls=%async_computation.1 | async-start | bytes 5570560 | tf_op jit(solution)/shard_map/all_gather | solution.py:63
  141.1 7.5 %copy-start.4 = (f32[2,38]{1,0:T(2,128)S(1)}, f32[2,38]{1,0:T(2,128)}, u32[]{:S(2)}) copy-start(f32[2,38]{1,0:T(2,128)} %param.14) | copy-start | bytes 916
  141.6 7.0 %collective-permute-start = (f32[38,1,128]{2,1,0:T(1,128)S(1)}, f32[38,1,128]{2,1,0:T(1,128)S(1)}, u32[]{:S(2)}, u32[]{:S(2)}) collective-permute-start(f32[38,1,128]{2,1,0:T(1,128)S(1)} %get-tuple-element.14), channel_id=1, source_target_pairs={{16,0},{32,16},{48,32},{64,48},{80,64},{96,80},{112,96},{128,112},... | collective-permute-start | bytes 58376 | tf_op jit(solution)/shard_map/ppermute | solution.py:20
  144.3 5.1 %collective-permute-start.1 = (f32[38,1,128]{2,1,0:T(1,128)S(1)}, f32[38,1,128]{2,1,0:T(1,128)S(1)}, u32[]{:S(2)}, u32[]{:S(2)}) collective-permute-start(f32[38,1,128]{2,1,0:T(1,128)S(1)} %get-tuple-element.15), channel_id=1, source_target_pairs={{0,16},{16,32},{32,48},{48,64},{64,80},{80,96},{96,112},{112,128},... | collective-permute-start | bytes 58376 | tf_op jit(solution)/shard_map/ppermute | solution.py:17
  150.0 6.1 %collective-permute-start.2 = (f32[38,1,128]{2,1,0:T(1,128)S(1)}, f32[38,1,128]{2,1,0:T(1,128)S(1)}, u32[]{:S(2)}, u32[]{:S(2)}) collective-permute-start(f32[38,1,128]{2,1,0:T(1,128)S(1)} %get-tuple-element.12), channel_id=1, source_target_pairs={{16,0},{32,16},{48,32},{64,48},{80,64},{96,80},{112,96},{128,112},... | collective-permute-start | bytes 58376 | tf_op jit(solution)/shard_map/ppermute | solution.py:20
  151.9 5.1 %collective-permute-start.3 = (f32[38,1,128]{2,1,0:T(1,128)S(1)}, f32[38,1,128]{2,1,0:T(1,128)S(1)}, u32[]{:S(2)}, u32[]{:S(2)}) collective-permute-start(f32[38,1,128]{2,1,0:T(1,128)S(1)} %get-tuple-element.13), channel_id=1, source_target_pairs={{0,16},{16,32},{32,48},{48,64},{64,80},{80,96},{96,112},{112,128},... | collective-permute-start | bytes 58376 | tf_op jit(solution)/shard_map/ppermute | solution.py:17
  157.6 6.1 %collective-permute-start.4 = (f32[38,1,128]{2,1,0:T(1,128)S(1)}, f32[38,1,128]{2,1,0:T(1,128)S(1)}, u32[]{:S(2)}, u32[]{:S(2)}) collective-permute-start(f32[38,1,128]{2,1,0:T(1,128)S(1)} %get-tuple-element.10), channel_id=1, source_target_pairs={{16,0},{32,16},{48,32},{64,48},{80,64},{96,80},{112,96},{128,112},... | collective-permute-start | bytes 58376 | tf_op jit(solution)/shard_map/ppermute | solution.py:20
  159.5 5.1 %collective-permute-start.5 = (f32[38,1,128]{2,1,0:T(1,128)S(1)}, f32[38,1,128]{2,1,0:T(1,128)S(1)}, u32[]{:S(2)}, u32[]{:S(2)}) collective-permute-start(f32[38,1,128]{2,1,0:T(1,128)S(1)} %get-tuple-element.11), channel_id=1, source_target_pairs={{0,16},{16,32},{32,48},{48,64},{64,80},{80,96},{96,112},{112,128},... | collective-permute-start | bytes 58376 | tf_op jit(solution)/shard_map/ppermute | solution.py:17
  166.2 74.8 %copy-start.3 = (bf16[38,608]{1,0:T(8,128)(2,1)S(1)}, bf16[38,608]{1,0:T(8,128)(2,1)}, u32[]{:S(2)}) copy-start(bf16[38,608]{1,0:T(8,128)(2,1)} %param.15) | copy-start | bytes 138628
Sparse Core Ops, SparseCore 0:
  166.3 68.8 all-gather.2
where the time goes:
time: 253 us; the launch traced here: 252 us
  waiting for transfers between devices  170 us (67%)
  starting transfers between devices  36.2 us (14%)
  local copies, waits for them, and re-layouts  22.4 us (9%)
  between operations  13.6 us (5%)
  other arithmetic  5.22 us (2%)
  matrix products  4.96 us (2%)
    all_to_all x1, waiting for transfers between devices, on_device(): lax.all_to_all(outgoing, 'swath', split_axis=0, concat_axis=0, tiled=True)  97.9 us
    all_gather x1, waiting for transfers between devices, on_device(): lax.all_gather(smoothed, 'chan', axis=0, tiled=True)  69 us
    all_to_all x1, starting transfers between devices, on_device(): lax.all_to_all(outgoing, 'swath', split_axis=0, concat_axis=0, tiled=True)  16.9 us
    gather x1, local copies, waits for them, and re-layouts, on_device(): grid_profiles[slot_rows]  14.6 us
    ppermute x3, starting transfers between devices, extended_2(): lax.ppermute(lax.slice_in_dim(block, block.shape[dim] - width, None, axis...  12.6 us
    unnamed x18, local copies, waits for them, and re-layouts  7.56 us
    ppermute x3, starting transfers between devices, extended_2(): lax.ppermute(lax.slice_in_dim(block, 0, width, axis=dim), axis, backward)  6.62 us
  transfers between devices with their start and end apart: 8, of which 5 were waited for; matrix products, arithmetic and copies ran while one was open for 0% of the time, Pallas kernels for 0%

commit v1 on v0

--- a/solution.py
+++ b/solution.py
@@ -1,12 +1,24 @@
+import functools
 import math
 import jax
 import jax.numpy as jnp
 from jax import lax
 from jax.sharding import PartitionSpec as P
+from jax.lax import all_to_all, axis_size
 
 XTRACK = 128
 NANG = 8
 max_zenith = math.pi / 3.0
+
+
+def pass_field_now(u_in, mesh_dim):
+    b_next = jnp.stack([u_in for _ in range(axis_size(mesh_dim))])
+    y = all_to_all(b_next, axis_name=mesh_dim, split_axis=0, concat_axis=0)
+    after = jnp.concatenate(y, 0)
+    return after
+
+
+reach_points = functools.partial(pass_field_now, mesh_dim="chan")
 
 
 def extended_2(block, sides, width):
@@ -58,11 +70,7 @@
     for sweep in range(3):
         smooth_field = diffuse_once(line_rims(smooth_field), along_rate, cross_rate)
     smoothed = smooth_field.reshape(own_chan, pixel_count).astype(jnp.bfloat16)
-    return jnp.dot(
-        factor,
-        lax.all_gather(smoothed, "chan", axis=0, tiled=True),
-        preferred_element_type=jnp.float32,
-    )
+    return jnp.dot(factor, reach_points(smoothed), preferred_element_type=jnp.float32)
 
 
 def solution(mesh):

time: 253 us -> 238 us (0.941)
  waiting for transfers between devices: 170 us -> 100 us
  blocking collectives: 0 us -> 67.9 us
  between operations: 13.6 us -> 0.26 us
    all_gather x1 -> x0, waiting for transfers between devices: 69 us -> none  [on_device(): lax.all_gather(smoothed, 'chan', axis=0, tiled=True)]
    all_to_all x0 -> x1, blocking collectives: none -> 67.9 us  [pass_field_now(): y = all_to_all(b_next, axis_name=mesh_dim, split_axis=0, concat_axis=0)]
    unnamed x18, local copies, waits for them, and re-layouts: 7.56 us -> 1.12 us
    reshape x0 -> x1, local copies, waits for them, and re-layouts: none -> 5.75 us  [pass_field_now(): after = jnp.concatenate(y, 0)]
  transfers between devices with their start and end apart: 8 -> 7, of which waited for: 5 -> 4; matrix products, arithmetic and copies ran while one was open for 0% -> 0% of each run, Pallas kernels for 0% -> 0%
where the time goes in v1:
time: 238 us; the launch traced here: 237 us
  waiting for transfers between devices  100 us (42%)
  blocking collectives  67.9 us (29%)
  starting transfers between devices  36.1 us (15%)
  local copies, waits for them, and re-layouts  22.4 us (9%)
  other arithmetic  5.24 us (2%)
  matrix products  4.97 us (2%)
    all_to_all x1, waiting for transfers between devices, on_device(): lax.all_to_all(outgoing, 'swath', split_axis=0, concat_axis=0, tiled=True)  97.9 us
    all_to_all x1, blocking collectives, pass_field_now(): y = all_to_all(b_next, axis_name=mesh_dim, split_axis=0, concat_axis=0)  67.9 us
    all_to_all x1, starting transfers between devices, on_device(): lax.all_to_all(outgoing, 'swath', split_axis=0, concat_axis=0, tiled=True)  16.9 us
    gather x1, local copies, waits for them, and re-layouts, on_device(): grid_profiles[slot_rows]  14.6 us
    ppermute x3, starting transfers between devices, extended_2(): lax.ppermute(lax.slice_in_dim(block, block.shape[dim] - width, None, axis...  12.6 us
    ppermute x3, starting transfers between devices, extended_2(): lax.ppermute(lax.slice_in_dim(block, 0, width, axis=dim), axis, backward)  6.62 us
    reshape x1, local copies, waits for them, and re-layouts, pass_field_now(): after = jnp.concatenate(y, 0)  5.75 us
  transfers between devices with their start and end apart: 7, of which 4 were waited for; matrix products, arithmetic and copies ran while one was open for 0% of the time, Pallas kernels for 0%

profile of v1, /device:TPU:1, one launch (start us, length us, event | category | flops | bytes accessed | tf_op | source)
XLA Modules:
  0.0 237.3 jit_solution(8014873120014591431)
XLA Ops:
  0.0 0.0 copy-start
  0.0 0.8 iota_compare_fusion
  0.8 0.7 fusion.29
  1.5 0.0 copy-done
  1.5 14.6 %gather_fusion = bf16[4096,256]{1,0:T(8,128)(2,1)S(1)} fusion(bf16[1024,256]{1,0:T(8,128)(2,1)S(1)} %copy-done, s32[4096]{0:T(1024)S(1)} %fusion.29), kind=kCustom, calls=%fused_computation | custom fusion | bytes 4210688 | tf_op jit(solution)/shard_map/gather | solution.py:57
  16.1 1.7 broadcast_select_fusion
  17.8 0.0 copy-start.1
  17.8 16.9 %all-to-all-start = ((bf16[32,128,256]{2,1,0:T(8,128)(2,1)}), bf16[32,128,256]{2,1,0:T(8,128)(2,1)S(1)}, u32[]{:S(2)}, u32[]{:S(2)}) async-start(bf16[32,128,256]{2,1,0:T(8,128)(2,1)} %broadcast_select_fusion), calls=%async_computation | async-start | bytes 4194304 | tf_op jit(solution)/shard_map/all_to_all | solution.py:58
  34.7 0.0 copy-done.1
  34.7 0.0 copy-start.5
  34.8 0.0 copy-start.2
  34.8 0.1 copy.9
  34.9 0.5 copy-done.5
  35.4 97.9 %all-to-all-done = bf16[32,128,256]{2,1,0:T(8,128)(2,1)S(1)} async-done(((bf16[32,128,256]{2,1,0:T(8,128)(2,1)}), bf16[32,128,256]{2,1,0:T(8,128)(2,1)S(1)}, u32[]{:S(2)}, u32[]{:S(2)}) %all-to-all-start) | async-done | bytes 2097184 | tf_op jit(solution)/shard_map/all_to_all | solution.py:58
  133.3 0.0 copy-done.2
  133.3 0.8 convolution_bitcast_fusion
  134.1 0.2 fusion.31
  134.3 0.1 copy.10
  134.4 0.1 copy.12
  134.6 0.0 copy-start.4
  134.6 0.1 copy.11
  134.7 0.3 fusion.14
  135.0 2.8 %collective-permute-start = (f32[38,1,128]{2,1,0:T(1,128)S(1)}, f32[38,1,128]{2,1,0:T(1,128)S(1)}, u32[]{:S(2)}, u32[]{:S(2)}) collective-permute-start(f32[38,1,128]{2,1,0:T(1,128)S(1)} %get-tuple-element.14), channel_id=1, source_target_pairs={{16,0},{32,16},{48,32},{64,48},{80,64},{96,80},{112,96},{128,112},... | collective-permute-start | bytes 58376 | tf_op jit(solution)/shard_map/ppermute | solution.py:32
  137.8 4.2 %collective-permute-start.1 = (f32[38,1,128]{2,1,0:T(1,128)S(1)}, f32[38,1,128]{2,1,0:T(1,128)S(1)}, u32[]{:S(2)}, u32[]{:S(2)}) collective-permute-start(f32[38,1,128]{2,1,0:T(1,128)S(1)} %get-tuple-element.15), channel_id=1, source_target_pairs={{0,16},{16,32},{32,48},{48,64},{64,80},{80,96},{96,112},{112,128},... | collective-permute-start | bytes 58376 | tf_op jit(solution)/shard_map/ppermute | solution.py:29
  142.1 0.0 copy-done.4
  142.1 0.0 collective-permute-done
  142.1 0.8 collective-permute-done.1
  142.9 0.5 fusion.3
  143.5 1.9 collective-permute-start.2
  145.4 4.2 %collective-permute-start.3 = (f32[38,1,128]{2,1,0:T(1,128)S(1)}, f32[38,1,128]{2,1,0:T(1,128)S(1)}, u32[]{:S(2)}, u32[]{:S(2)}) collective-permute-start(f32[38,1,128]{2,1,0:T(1,128)S(1)} %get-tuple-element.13), channel_id=1, source_target_pairs={{0,16},{16,32},{32,48},{48,64},{64,80},{80,96},{96,112},{112,128},... | collective-permute-start | bytes 58376 | tf_op jit(solution)/shard_map/ppermute | solution.py:29
  149.6 0.0 collective-permute-done.2
  149.7 0.9 collective-permute-done.3
  150.5 0.5 fusion.7
  151.1 1.9 collective-permute-start.4
  153.0 4.2 %collective-permute-start.5 = (f32[38,1,128]{2,1,0:T(1,128)S(1)}, f32[38,1,128]{2,1,0:T(1,128)S(1)}, u32[]{:S(2)}, u32[]{:S(2)}) collective-permute-start(f32[38,1,128]{2,1,0:T(1,128)S(1)} %get-tuple-element.11), channel_id=1, source_target_pairs={{0,16},{16,32},{32,48},{48,64},{64,80},{80,96},{96,112},{112,128},... | collective-permute-start | bytes 58376 | tf_op jit(solution)/shard_map/ppermute | solution.py:29
  157.2 0.0 collective-permute-done.4
  157.2 0.9 collective-permute-done.5
  158.1 0.6 fusion.12
  158.7 0.1 copy.13
  158.9 0.6 stack.2
  159.5 67.9 %all_to_all.10 = bf16[16,38,4096]{2,1,0:T(8,128)(2,1)} all-to-all(bf16[16,38,4096]{2,1,0:T(8,128)(2,1)S(1)} %stack.2), channel_id=1, replica_groups=mesh['swath'=32,'chan'=16] {'chan'}, dimensions={0} | all-to-all | bytes 9961472 | tf_op jit(solution)/shard_map/all_to_all | solution.py:16
  227.4 0.0 copy-start.3
  227.4 5.7 %reshape.83 = bf16[608,4096]{1,0:T(8,128)(2,1)} reshape(bf16[16,38,4096]{2,1,0:T(8,128)(2,1)} %all_to_all.10) | data formatting | bytes 9961472 | tf_op jit(solution)/shard_map/reshape | solution.py:17
  233.1 0.0 copy-done.3
  233.1 4.2 %convolution_bitcast_fusion.1 = f32[38,4096]{1,0:T(8,128)} fusion(bf16[608,4096]{1,0:T(8,128)(2,1)} %reshape.83, bf16[38,608]{1,0:T(8,128)(2,1)S(1)} %copy-done.3), kind=kOutput, calls=%fused_computation.2 | convolution fusion | flops 189267968 | bytes 5649536 | tf_op jit(solution)/shard_map/dot_general | solution.py:73
  (7 shorter events, 0.2 us)
Async XLA Ops:
  0.0 1.5 copy-start
  17.8 16.9 %copy-start.1 = (bf16[38,4096]{1,0:T(8,128)(2,1)S(1)}, bf16[38,4096]{1,0:T(8,128)(2,1)}, u32[]{:S(2)}) copy-start(bf16[38,4096]{1,0:T(8,128)(2,1)} %param.13) | copy-start | bytes 933892
  17.8 115.5 %all-to-all-start = ((bf16[32,128,256]{2,1,0:T(8,128)(2,1)}), bf16[32,128,256]{2,1,0:T(8,128)(2,1)S(1)}, u32[]{:S(2)}, u32[]{:S(2)}) async-start(bf16[32,128,256]{2,1,0:T(8,128)(2,1)} %broadcast_select_fusion), calls=%async_computation | async-start | bytes 4194304 | tf_op jit(solution)/shard_map/all_to_all | solution.py:58
  34.7 0.7 copy-start.5
  34.8 98.6 %copy-start.2 = (bf16[3,256,38]{1,2,0:T(8,128)(2,1)S(1)}, bf16[3,256,38]{1,2,0:T(8,128)(2,1)}, u32[]{:S(2)}) copy-start(bf16[3,256,38]{1,2,0:T(8,128)(2,1)} %param.12) | copy-start | bytes 175108
  134.6 7.5 %copy-start.4 = (f32[2,38]{1,0:T(2,128)S(1)}, f32[2,38]{1,0:T(2,128)}, u32[]{:S(2)}) copy-start(f32[2,38]{1,0:T(2,128)} %param.14) | copy-start | bytes 916
  135.0 7.0 %collective-permute-start = (f32[38,1,128]{2,1,0:T(1,128)S(1)}, f32[38,1,128]{2,1,0:T(1,128)S(1)}, u32[]{:S(2)}, u32[]{:S(2)}) collective-permute-start(f32[38,1,128]{2,1,0:T(1,128)S(1)} %get-tuple-element.14), channel_id=1, source_target_pairs={{16,0},{32,16},{48,32},{64,48},{80,64},{96,80},{112,96},{128,112},... | collective-permute-start | bytes 58376 | tf_op jit(solution)/shard_map/ppermute | solution.py:32
  137.8 5.1 %collective-permute-start.1 = (f32[38,1,128]{2,1,0:T(1,128)S(1)}, f32[38,1,128]{2,1,0:T(1,128)S(1)}, u32[]{:S(2)}, u32[]{:S(2)}) collective-permute-start(f32[38,1,128]{2,1,0:T(1,128)S(1)} %get-tuple-element.15), channel_id=1, source_target_pairs={{0,16},{16,32},{32,48},{48,64},{64,80},{80,96},{96,112},{112,128},... | collective-permute-start | bytes 58376 | tf_op jit(solution)/shard_map/ppermute | solution.py:29
  143.5 6.1 %collective-permute-start.2 = (f32[38,1,128]{2,1,0:T(1,128)S(1)}, f32[38,1,128]{2,1,0:T(1,128)S(1)}, u32[]{:S(2)}, u32[]{:S(2)}) collective-permute-start(f32[38,1,128]{2,1,0:T(1,128)S(1)} %get-tuple-element.12), channel_id=1, source_target_pairs={{16,0},{32,16},{48,32},{64,48},{80,64},{96,80},{112,96},{128,112},... | collective-permute-start | bytes 58376 | tf_op jit(solution)/shard_map/ppermute | solution.py:32
  145.4 5.1 %collective-permute-start.3 = (f32[38,1,128]{2,1,0:T(1,128)S(1)}, f32[38,1,128]{2,1,0:T(1,128)S(1)}, u32[]{:S(2)}, u32[]{:S(2)}) collective-permute-start(f32[38,1,128]{2,1,0:T(1,128)S(1)} %get-tuple-element.13), channel_id=1, source_target_pairs={{0,16},{16,32},{32,48},{48,64},{64,80},{80,96},{96,112},{112,128},... | collective-permute-start | bytes 58376 | tf_op jit(solution)/shard_map/ppermute | solution.py:29
  151.1 6.1 %collective-permute-start.4 = (f32[38,1,128]{2,1,0:T(1,128)S(1)}, f32[38,1,128]{2,1,0:T(1,128)S(1)}, u32[]{:S(2)}, u32[]{:S(2)}) collective-permute-start(f32[38,1,128]{2,1,0:T(1,128)S(1)} %get-tuple-element.10), channel_id=1, source_target_pairs={{16,0},{32,16},{48,32},{64,48},{80,64},{96,80},{112,96},{128,112},... | collective-permute-start | bytes 58376 | tf_op jit(solution)/shard_map/ppermute | solution.py:32
  153.0 5.1 %collective-permute-start.5 = (f32[38,1,128]{2,1,0:T(1,128)S(1)}, f32[38,1,128]{2,1,0:T(1,128)S(1)}, u32[]{:S(2)}, u32[]{:S(2)}) collective-permute-start(f32[38,1,128]{2,1,0:T(1,128)S(1)} %get-tuple-element.11), channel_id=1, source_target_pairs={{0,16},{16,32},{32,48},{48,64},{64,80},{80,96},{96,112},{112,128},... | collective-permute-start | bytes 58376 | tf_op jit(solution)/shard_map/ppermute | solution.py:29
  227.4 5.8 %copy-start.3 = (bf16[38,608]{1,0:T(8,128)(2,1)S(1)}, bf16[38,608]{1,0:T(8,128)(2,1)}, u32[]{:S(2)}) copy-start(bf16[38,608]{1,0:T(8,128)(2,1)} %param.15) | copy-start | bytes 138628
